TPU v7x, 32 devices: a whole 2x2x4 slice. The times are simulated.
32 devices in a mesh: grp: 4 (over x, core), mem: 8 (over z, y).
Axes of the slice: x: 2, y: 2, z: 4, core: 2. Of those that a mesh axis runs over, the one named last changes fastest.
Arguments:
- history: bfloat16 [16384, 256], P(('grp', 'mem')), may hold values from -6 to 6
- tiles: bfloat16 [20480, 128, 128], P(('grp', 'mem')), may hold values from -0.0390625 to 0.0390625
- tile_row: int32 [20480], P(('grp', 'mem')), may hold values from 0 to 31
- tile_col: int32 [20480], P(('grp', 'mem')), may hold values from 0 to 31
- weight: bfloat16 [256, 256], replicated, may hold values from -0.375 to 0.375
- bias: float32 [256], replicated, may hold values from -3 to 3
- cotangent: bfloat16 [16384, 256], P(('grp', 'mem')), may hold values from -0.046875 to 0.046875
Outputs:
- activation: bfloat16 [16384, 256], P(('grp', 'mem'))
- weight_grad: float32 [256, 256], replicated
- bias_grad: float32 [256], replicated
All inputs are finite; a program needn't handle non-finite values.
Results may differ from a plain program's by a relative error of at most 0.012.
Values may be sent and summed in bfloat16 or wider, within the bound.
No kernel may reach another device: no remote copies, remote signals or barrier semaphores. Data moves between devices by JAX's collectives and lax.ppermute only.
A program may use at most 128 MiB of HBM per device.

v0:
```python
import math
import jax
import jax.numpy as jnp
from jax import lax
from jax.sharding import PartitionSpec as P


def per_device(history, tiles, tile_row, tile_col, weight, bias, cotangent):
    own_rows = history.shape[0]
    block = tiles.shape[1]
    width = history.shape[1]
    group = lax.all_gather(history, "mem", axis=0, tiled=True)
    nblk = group.shape[0] // block
    flat_blocks = group.reshape(nblk, block * width)
    step = math.gcd(tiles.shape[0], 64)
    count = tiles.shape[0] // step
    block_ids = lax.broadcasted_iota(jnp.int32, (step, nblk), 1)

    def accumulate(index, dense):
        start = index * step
        piece = lax.dynamic_slice_in_dim(tiles, start, step, 0)
        rows = lax.dynamic_slice_in_dim(tile_row, start, step, 0)
        cols = lax.dynamic_slice_in_dim(tile_col, start, step, 0)
        col_table = (cols[:, None] == block_ids).astype(jnp.bfloat16)
        row_table = (rows[:, None] == block_ids).astype(jnp.bfloat16)
        picked = jnp.dot(col_table, flat_blocks, preferred_element_type=jnp.float32).astype(
            jnp.bfloat16
        )
        picked = picked.reshape(step, block, width)
        part = jnp.einsum("tij,tjh->tih", piece, picked, preferred_element_type=jnp.float32)
        part = part.reshape(step, block * width)
        upper = part.astype(jnp.bfloat16)
        lower = (part - upper.astype(jnp.float32)).astype(jnp.bfloat16)
        contract = (((0,), (0,)), ((), ()))
        added = lax.dot_general(row_table, upper, contract, preferred_element_type=jnp.float32)
        added = added + lax.dot_general(
            row_table, lower, contract, preferred_element_type=jnp.float32
        )
        return dense + added

    dense = lax.fori_loop(0, count, accumulate, jnp.zeros((nblk, block * width), jnp.float32))
    flat = dense.reshape(nblk * block, width)
    total = lax.psum(flat, "mem")
    summed = lax.dynamic_slice_in_dim(total, lax.axis_index("mem") * own_rows, own_rows, 0)
    merged = summed.astype(jnp.bfloat16)
    pre = jnp.dot(merged, weight, preferred_element_type=jnp.float32) + bias
    sig = jax.nn.sigmoid(pre)
    activation = (pre * sig).astype(jnp.bfloat16)
    slope = sig * (1.0 + pre * (1.0 - sig))
    masked = (cotangent.astype(jnp.float32) * slope).astype(jnp.bfloat16)
    local_grad = lax.dot_general(
        merged, masked, (((0,), (0,)), ((), ())), preferred_element_type=jnp.float32
    )
    local_bias = jnp.sum(masked.astype(jnp.float32), axis=0)
    weight_grad, bias_grad = lax.psum((local_grad, local_bias), ("grp", "mem"))
    return (activation, weight_grad, bias_grad)


def solution(mesh):
    placed = (
        P(("grp", "mem"), None),
        P(("grp", "mem"), None, None),
        P(("grp", "mem")),
        P(("grp", "mem")),
        P(),
        P(),
        P(("grp", "mem"), None),
    )
    return jax.shard_map(
        per_device,
        mesh=mesh,
        in_specs=placed,
        out_specs=(P(("grp", "mem"), None), P(), P()),
        check_vma=False,
    )
```

profile of v0, /device:TPU:0, one launch (start us, length us, event | category | flops | bytes accessed | tf_op | source)
XLA Modules:
  0.0 637.3 jit_solution(10937932440289297246)
XLA Ops:
  8.0 54.0 %all-gather.2.cloned.1.call-done = bf16[4096,256]{1,0:T(8,128)(2,1)} async-done(((bf16[512,256]{1,0:T(8,128)(2,1)}), bf16[4096,256]{1,0:T(8,128)(2,1)}) %all-gather.2.cloned.1.call-update) | async-done | bytes 2097168 | tf_op jit(solution)/shard_map/all_gather | solution.py:12
  64.8 266.7 %while.15 = (s32[]{:T(128)}, f32[32,32768]{1,0:T(8,128)}, s32[640]{0:T(1024)}, bf16[640,128,128]{2,1,0:T(8,128)(2,1)}, s32[640]{0:T(1024)}, /*index=5*/bf16[32,3...) while((s32[]{:T(128)}, f32[32,32768]{1,0:T(8,128)}, ...), condition=%wide.region_1.0_spmd.clone.clone, body=%wide.region_0.0_spmd.clone.clone.sunk | while | flops 955258880 | bytes 113248200 | solution.py:41
  70.9 4.7 copy.15
  76.4 3.5 fusion.31
  80.2 10.3 %fusion.32 = f32[32,32768]{1,0:T(8,128)} fusion(f32[32,32768]{1,0:T(8,128)} %fusion.31, f32[64,32768]{1,0:T(8,128)} %bitcast.21, f32[32,32768]{1,0:T(8,128)} %get-tuple-element.235, pred[]{:T(512)S(6)} %compare.3, s32[64]{0:T(128)S(1)} %dynamic_slice.43), kind=kOutput, calls=%fused_computation.3.clone.1 | convolution fusion | flops 145754112 | bytes 20971776 | tf_op jit(solution)/shard_map/while/body/eval_jaxpr/dot_general | solution.py:36
  96.5 4.7 copy.15
  102.0 3.5 fusion.31
  105.8 11.5 %fusion.32 = f32[32,32768]{1,0:T(8,128)} fusion(f32[32,32768]{1,0:T(8,128)} %fusion.31, f32[64,32768]{1,0:T(8,128)} %bitcast.21, f32[32,32768]{1,0:T(8,128)} %get-tuple-element.235, pred[]{:T(512)S(6)} %compare.3, s32[64]{0:T(128)S(1)} %dynamic_slice.43), kind=kOutput, calls=%fused_computation.3.clone.1 | convolution fusion | flops 145754112 | bytes 20971776 | tf_op jit(solution)/shard_map/while/body/eval_jaxpr/dot_general | solution.py:36
  123.3 4.7 copy.15
  128.8 3.5 fusion.31
  132.6 11.5 %fusion.32 = f32[32,32768]{1,0:T(8,128)} fusion(f32[32,32768]{1,0:T(8,128)} %fusion.31, f32[64,32768]{1,0:T(8,128)} %bitcast.21, f32[32,32768]{1,0:T(8,128)} %get-tuple-element.235, pred[]{:T(512)S(6)} %compare.3, s32[64]{0:T(128)S(1)} %dynamic_slice.43), kind=kOutput, calls=%fused_computation.3.clone.1 | convolution fusion | flops 145754112 | bytes 20971776 | tf_op jit(solution)/shard_map/while/body/eval_jaxpr/dot_general | solution.py:36
  150.1 4.7 copy.15
  155.6 3.5 fusion.31
  159.4 11.5 %fusion.32 = f32[32,32768]{1,0:T(8,128)} fusion(f32[32,32768]{1,0:T(8,128)} %fusion.31, f32[64,32768]{1,0:T(8,128)} %bitcast.21, f32[32,32768]{1,0:T(8,128)} %get-tuple-element.235, pred[]{:T(512)S(6)} %compare.3, s32[64]{0:T(128)S(1)} %dynamic_slice.43), kind=kOutput, calls=%fused_computation.3.clone.1 | convolution fusion | flops 145754112 | bytes 20971776 | tf_op jit(solution)/shard_map/while/body/eval_jaxpr/dot_general | solution.py:36
  176.8 4.7 copy.15
  182.4 3.5 fusion.31
  186.1 11.5 %fusion.32 = f32[32,32768]{1,0:T(8,128)} fusion(f32[32,32768]{1,0:T(8,128)} %fusion.31, f32[64,32768]{1,0:T(8,128)} %bitcast.21, f32[32,32768]{1,0:T(8,128)} %get-tuple-element.235, pred[]{:T(512)S(6)} %compare.3, s32[64]{0:T(128)S(1)} %dynamic_slice.43), kind=kOutput, calls=%fused_computation.3.clone.1 | convolution fusion | flops 145754112 | bytes 20971776 | tf_op jit(solution)/shard_map/while/body/eval_jaxpr/dot_general | solution.py:36
  203.6 4.7 copy.15
  209.2 3.5 fusion.31
  212.9 11.5 %fusion.32 = f32[32,32768]{1,0:T(8,128)} fusion(f32[32,32768]{1,0:T(8,128)} %fusion.31, f32[64,32768]{1,0:T(8,128)} %bitcast.21, f32[32,32768]{1,0:T(8,128)} %get-tuple-element.235, pred[]{:T(512)S(6)} %compare.3, s32[64]{0:T(128)S(1)} %dynamic_slice.43), kind=kOutput, calls=%fused_computation.3.clone.1 | convolution fusion | flops 145754112 | bytes 20971776 | tf_op jit(solution)/shard_map/while/body/eval_jaxpr/dot_general | solution.py:36
  230.4 4.7 copy.15
  239.7 11.5 %fusion.32 = f32[32,32768]{1,0:T(8,128)} fusion(f32[32,32768]{1,0:T(8,128)} %fusion.31, f32[64,32768]{1,0:T(8,128)} %bitcast.21, f32[32,32768]{1,0:T(8,128)} %get-tuple-element.235, pred[]{:T(512)S(6)} %compare.3, s32[64]{0:T(128)S(1)} %dynamic_slice.43), kind=kOutput, calls=%fused_computation.3.clone.1 | convolution fusion | flops 145754112 | bytes 20971776 | tf_op jit(solution)/shard_map/while/body/eval_jaxpr/dot_general | solution.py:36
  257.2 4.7 copy.15
  266.5 11.5 %fusion.32 = f32[32,32768]{1,0:T(8,128)} fusion(f32[32,32768]{1,0:T(8,128)} %fusion.31, f32[64,32768]{1,0:T(8,128)} %bitcast.21, f32[32,32768]{1,0:T(8,128)} %get-tuple-element.235, pred[]{:T(512)S(6)} %compare.3, s32[64]{0:T(128)S(1)} %dynamic_slice.43), kind=kOutput, calls=%fused_computation.3.clone.1 | convolution fusion | flops 145754112 | bytes 20971776 | tf_op jit(solution)/shard_map/while/body/eval_jaxpr/dot_general | solution.py:36
  284.0 4.7 copy.15
  293.3 11.5 %fusion.32 = f32[32,32768]{1,0:T(8,128)} fusion(f32[32,32768]{1,0:T(8,128)} %fusion.31, f32[64,32768]{1,0:T(8,128)} %bitcast.21, f32[32,32768]{1,0:T(8,128)} %get-tuple-element.235, pred[]{:T(512)S(6)} %compare.3, s32[64]{0:T(128)S(1)} %dynamic_slice.43), kind=kOutput, calls=%fused_computation.3.clone.1 | convolution fusion | flops 145754112 | bytes 20971776 | tf_op jit(solution)/shard_map/while/body/eval_jaxpr/dot_general | solution.py:36
  310.8 4.7 copy.15
  320.1 11.5 %fusion.32 = f32[32,32768]{1,0:T(8,128)} fusion(f32[32,32768]{1,0:T(8,128)} %fusion.31, f32[64,32768]{1,0:T(8,128)} %bitcast.21, f32[32,32768]{1,0:T(8,128)} %get-tuple-element.235, pred[]{:T(512)S(6)} %compare.3, s32[64]{0:T(128)S(1)} %dynamic_slice.43), kind=kOutput, calls=%fused_computation.3.clone.1 | convolution fusion | flops 145754112 | bytes 20971776 | tf_op jit(solution)/shard_map/while/body/eval_jaxpr/dot_general | solution.py:36
  331.6 4.9 reshape.30
  336.4 165.1 %all-reduce.4 = bf16[4096,256]{1,0:T(8,128)(2,1)S(1)} all-reduce(f32[4096,256]{1,0:T(8,128)} %reshape.30), channel_id=1, replica_groups=mesh['grp'=4,'mem'=8] {'mem'}, use_global_device_ids=true, to_apply=%region_2.0 | all-reduce | flops 1048576 | bytes 6291456 | tf_op jit(solution)/shard_map/psum | solution.py:43
  503.7 39.3 %psum.23 = f32[256]{0:T(256)} all-reduce(f32[256]{0:T(256)S(1)} %get-tuple-element.184), channel_id=1, replica_groups=mesh['grp'=4,'mem'=8] {'grp','mem'}, use_global_device_ids=true, to_apply=%region_5.0 | all-reduce | flops 256 | bytes 2048 | tf_op jit(solution)/shard_map/psum | solution.py:55
  543.1 85.7 %all-reduce.3.cloned.1.call-done = f32[256,256]{1,0:T(8,128)} async-done(((f32[256,256]{1,0:T(8,128)}), f32[256,256]{1,0:T(8,128)}) %all-reduce.3.cloned.1.call-update) | async-done | bytes 262160 | tf_op jit(solution)/shard_map/psum | solution.py:55
  (89 shorter events, 92.3 us)
Async XLA Ops:
  7.2 494.4 %copy-start = (bf16[256,256]{1,0:T(8,128)(2,1)S(1)}, bf16[256,256]{1,0:T(8,128)(2,1)}, u32[]{:S(2)}) copy-start(bf16[256,256]{1,0:T(8,128)(2,1)} %param.13) | copy-start | bytes 393220
  7.2 54.8 %all-gather.2.cloned.1.call-start = ((), (), s32[]{:S(2)}) async-start(), calls=%async_computation | async-start | bytes 2359296 | tf_op jit(solution)/shard_map/all_gather | solution.py:12
  7.9 620.8 %all-reduce.3.cloned.1.call-start = ((), (), s32[]{:S(2)}) async-start(), calls=%async_computation.1 | async-start | bytes 524288 | tf_op jit(solution)/shard_map/psum | solution.py:55
  75.6 4.6 copy-start.1
  101.2 4.6 copy-start.1
  128.0 4.6 copy-start.1
  154.8 4.6 copy-start.1
  181.6 4.6 copy-start.1
  208.4 4.6 copy-start.1
  235.2 4.6 copy-start.1
  261.9 4.6 copy-start.1
  288.7 4.6 copy-start.1
  315.5 4.6 copy-start.1
  336.4 165.2 %copy-start.2 = (bf16[512,256]{1,0:T(8,128)(2,1)S(1)}, bf16[512,256]{1,0:T(8,128)(2,1)}, u32[]{:S(2)}) copy-start(bf16[512,256]{1,0:T(8,128)(2,1)} %param.15) | copy-start | bytes 786436
  336.4 165.2 %copy-start.3 = (f32[256]{0:T(256)S(1)}, f32[256]{0:T(256)}, u32[]{:S(2)}) copy-start(f32[256]{0:T(256)} %param.14) | copy-start | bytes 3076
Sparse Core Ops, SparseCore 0:
  10.1 51.7 all-gather.1
  503.9 124.8 all-reduce.2
where the time goes:
time: 639 us; the launch traced here: 637 us
  blocking collectives  204 us (32%)
  matrix products  191 us (30%)
  waiting for transfers between devices  140 us (22%)
  local copies, waits for them, and re-layouts  86.4 us (14%)
  between operations  14.1 us (2%)
    psum x1, blocking collectives, per_device(): total = lax.psum(flat, 'mem')  165 us
    dot_general x10, matrix products, accumulate(): lax.dot_general(row_table, lower, contract, preferred_element_type=jnp.fl...  113 us
    psum x1, waiting for transfers between devices, per_device(): weight_grad, bias_grad = lax.psum((local_grad, local_bias), ('grp', 'mem'))  85.7 us
    while x40, local copies, waits for them, and re-layouts  61.2 us
    all_gather x1, waiting for transfers between devices, per_device(): group = lax.all_gather(history, 'mem', axis=0, tiled=True)  54 us
    psum x1, blocking collectives, per_device(): weight_grad, bias_grad = lax.psum((local_grad, local_bias), ('grp', 'mem'))  39.3 us
    dot_general x10, matrix products, accumulate(): lax.dot_general(row_table, upper, contract, preferred_element_type=jnp.fl...  34.5 us
    dot_general x10, matrix products, accumulate(): jnp.einsum('tij,tjh->tih', piece, picked, preferred_element_type=jnp.floa...  28.5 us
  transfers between devices with their start and end apart: 2, of which 2 were waited for; matrix products, arithmetic and copies ran while one was open for 0% of the time, Pallas kernels for 0%

commit v1 on v0

--- a/solution.py
+++ b/solution.py
@@ -3,6 +3,15 @@
 import jax.numpy as jnp
 from jax import lax
 from jax.sharding import PartitionSpec as P
+
+
+def doubling_sum(x, name):
+    devices = lax.axis_size(name)
+    total, far = (x, 1)
+    while far < devices:
+        total = total + lax.ppermute(total, name, [(i, i ^ far) for i in range(devices)])
+        far = 2 * far
+    return total
 
 
 def per_device(history, tiles, tile_row, tile_col, weight, bias, cotangent):
@@ -40,7 +49,7 @@
 
     dense = lax.fori_loop(0, count, accumulate, jnp.zeros((nblk, block * width), jnp.float32))
     flat = dense.reshape(nblk * block, width)
-    total = lax.psum(flat, "mem")
+    total = doubling_sum(flat, "mem")
     summed = lax.dynamic_slice_in_dim(total, lax.axis_index("mem") * own_rows, own_rows, 0)
     merged = summed.astype(jnp.bfloat16)
     pre = jnp.dot(merged, weight, preferred_element_type=jnp.float32) + bias

time: 639 us -> 859 us (1.34)
  waiting for transfers between devices: 140 us -> 500 us
  blocking collectives: 204 us -> 38.5 us
  local copies, waits for them, and re-layouts: 86.4 us -> 108 us
    ppermute x0 -> x3, waiting for transfers between devices: none -> 357 us  [doubling_sum(): lax.ppermute(total, name, [(i, i ^ far) for i in range(devices)])]
    psum x1 -> x0, blocking collectives: 165 us -> none  [per_device(): total = lax.psum(flat, 'mem')]
    while x40, local copies, waits for them, and re-layouts: 61.2 us -> 82.3 us
  transfers between devices with their start and end apart: 2 -> 5, of which waited for: 2 -> 5; matrix products, arithmetic and copies ran while one was open for 0% -> 0% of each run, Pallas kernels for 0% -> 0%
where the time goes in v1:
time: 859 us; the launch traced here: 858 us
  waiting for transfers between devices  500 us (58%)
  matrix products  185 us (22%)
  local copies, waits for them, and re-layouts  108 us (13%)
  blocking collectives  38.5 us (4%)
  between operations  14.1 us (2%)
    ppermute x3, waiting for transfers between devices, doubling_sum(): lax.ppermute(total, name, [(i, i ^ far) for i in range(devices)])  357 us
    dot_general x10, matrix products, accumulate(): lax.dot_general(row_table, lower, contract, preferred_element_type=jnp.fl...  113 us
    psum x1, waiting for transfers between devices, per_device(): weight_grad, bias_grad = lax.psum((local_grad, local_bias), ('grp', 'mem'))  88.4 us
    while x40, local copies, waits for them, and re-layouts  82.3 us
    all_gather x1, waiting for transfers between devices, per_device(): group = lax.all_gather(history, 'mem', axis=0, tiled=True)  54 us
    psum x1, blocking collectives, per_device(): weight_grad, bias_grad = lax.psum((local_grad, local_bias), ('grp', 'mem'))  38.5 us
    dot_general x10, matrix products, accumulate(): jnp.einsum('tij,tjh->tih', piece, picked, preferred_element_type=jnp.floa...  28.5 us
    dot_general x10, matrix products, accumulate(): lax.dot_general(row_table, upper, contract, preferred_element_type=jnp.fl...  27.9 us
  transfers between devices with their start and end apart: 5, of which 5 were waited for; matrix products, arithmetic and copies ran while one was open for 0% of the time, Pallas kernels for 0%

profile of v1, /device:TPU:0, one launch (start us, length us, event | category | flops | bytes accessed | tf_op | source)
XLA Modules:
  0.0 857.6 jit_solution(5728018738325929931)
XLA Ops:
  8.0 54.0 %all-gather.2.cloned.1.call-done = bf16[4096,256]{1,0:T(8,128)(2,1)} async-done(((bf16[512,256]{1,0:T(8,128)(2,1)}), bf16[4096,256]{1,0:T(8,128)(2,1)}) %all-gather.2.cloned.1.call-update) | async-done | bytes 2097168 | tf_op jit(solution)/shard_map/all_gather | solution.py:21
  62.0 2.9 reshape.29
  64.8 281.1 %while.15 = (s32[]{:T(128)}, f32[32,32768]{1,0:T(8,128)}, s32[640]{0:T(1024)}, bf16[640,128,128]{2,1,0:T(8,128)(2,1)}, s32[640]{0:T(1024)}, /*index=5*/bf16[32,3...) while((s32[]{:T(128)}, f32[32,32768]{1,0:T(8,128)}, ...), condition=%wide.region_1.0_spmd.clone.clone, body=%wide.region_0.0_spmd.clone.clone.sunk | while | flops 955258880 | bytes 113248192 | solution.py:50
  68.0 2.9 fusion.31
  70.9 4.7 copy.15
  81.6 10.3 %fusion.33 = f32[32,32768]{1,0:T(8,128)} fusion(f32[32,32768]{1,0:T(8,128)} %fusion.32, f32[64,32768]{1,0:T(8,128)} %bitcast.23, f32[32,32768]{1,0:T(8,128)} %get-tuple-element.235, pred[]{:T(512)S(6)} %compare.3, s32[64]{0:T(128)S(1)} %dynamic_slice.44), kind=kOutput, calls=%fused_computation.3.clone.1 | convolution fusion | flops 145754112 | bytes 20971776 | tf_op jit(solution)/shard_map/while/body/eval_jaxpr/dot_general | solution.py:45
  97.9 4.7 copy.15
  108.7 11.5 %fusion.33 = f32[32,32768]{1,0:T(8,128)} fusion(f32[32,32768]{1,0:T(8,128)} %fusion.32, f32[64,32768]{1,0:T(8,128)} %bitcast.23, f32[32,32768]{1,0:T(8,128)} %get-tuple-element.235, pred[]{:T(512)S(6)} %compare.3, s32[64]{0:T(128)S(1)} %dynamic_slice.44), kind=kOutput, calls=%fused_computation.3.clone.1 | convolution fusion | flops 145754112 | bytes 20971776 | tf_op jit(solution)/shard_map/while/body/eval_jaxpr/dot_general | solution.py:45
  126.1 4.7 copy.15
  136.9 11.5 %fusion.33 = f32[32,32768]{1,0:T(8,128)} fusion(f32[32,32768]{1,0:T(8,128)} %fusion.32, f32[64,32768]{1,0:T(8,128)} %bitcast.23, f32[32,32768]{1,0:T(8,128)} %get-tuple-element.235, pred[]{:T(512)S(6)} %compare.3, s32[64]{0:T(128)S(1)} %dynamic_slice.44), kind=kOutput, calls=%fused_computation.3.clone.1 | convolution fusion | flops 145754112 | bytes 20971776 | tf_op jit(solution)/shard_map/while/body/eval_jaxpr/dot_general | solution.py:45
  151.5 2.9 fusion.31
  154.4 4.7 copy.15
  165.1 11.5 %fusion.33 = f32[32,32768]{1,0:T(8,128)} fusion(f32[32,32768]{1,0:T(8,128)} %fusion.32, f32[64,32768]{1,0:T(8,128)} %bitcast.23, f32[32,32768]{1,0:T(8,128)} %get-tuple-element.235, pred[]{:T(512)S(6)} %compare.3, s32[64]{0:T(128)S(1)} %dynamic_slice.44), kind=kOutput, calls=%fused_computation.3.clone.1 | convolution fusion | flops 145754112 | bytes 20971776 | tf_op jit(solution)/shard_map/while/body/eval_jaxpr/dot_general | solution.py:45
  182.6 4.7 copy.15
  193.3 11.5 %fusion.33 = f32[32,32768]{1,0:T(8,128)} fusion(f32[32,32768]{1,0:T(8,128)} %fusion.32, f32[64,32768]{1,0:T(8,128)} %bitcast.23, f32[32,32768]{1,0:T(8,128)} %get-tuple-element.235, pred[]{:T(512)S(6)} %compare.3, s32[64]{0:T(128)S(1)} %dynamic_slice.44), kind=kOutput, calls=%fused_computation.3.clone.1 | convolution fusion | flops 145754112 | bytes 20971776 | tf_op jit(solution)/shard_map/while/body/eval_jaxpr/dot_general | solution.py:45
  210.8 4.7 copy.15
  221.6 11.5 %fusion.33 = f32[32,32768]{1,0:T(8,128)} fusion(f32[32,32768]{1,0:T(8,128)} %fusion.32, f32[64,32768]{1,0:T(8,128)} %bitcast.23, f32[32,32768]{1,0:T(8,128)} %get-tuple-element.235, pred[]{:T(512)S(6)} %compare.3, s32[64]{0:T(128)S(1)} %dynamic_slice.44), kind=kOutput, calls=%fused_computation.3.clone.1 | convolution fusion | flops 145754112 | bytes 20971776 | tf_op jit(solution)/shard_map/while/body/eval_jaxpr/dot_general | solution.py:45
  239.0 4.7 copy.15
  249.8 11.5 %fusion.33 = f32[32,32768]{1,0:T(8,128)} fusion(f32[32,32768]{1,0:T(8,128)} %fusion.32, f32[64,32768]{1,0:T(8,128)} %bitcast.23, f32[32,32768]{1,0:T(8,128)} %get-tuple-element.235, pred[]{:T(512)S(6)} %compare.3, s32[64]{0:T(128)S(1)} %dynamic_slice.44), kind=kOutput, calls=%fused_computation.3.clone.1 | convolution fusion | flops 145754112 | bytes 20971776 | tf_op jit(solution)/shard_map/while/body/eval_jaxpr/dot_general | solution.py:45
  264.4 2.9 fusion.31
  267.3 4.7 copy.15
  278.0 11.5 %fusion.33 = f32[32,32768]{1,0:T(8,128)} fusion(f32[32,32768]{1,0:T(8,128)} %fusion.32, f32[64,32768]{1,0:T(8,128)} %bitcast.23, f32[32,32768]{1,0:T(8,128)} %get-tuple-element.235, pred[]{:T(512)S(6)} %compare.3, s32[64]{0:T(128)S(1)} %dynamic_slice.44), kind=kOutput, calls=%fused_computation.3.clone.1 | convolution fusion | flops 145754112 | bytes 20971776 | tf_op jit(solution)/shard_map/while/body/eval_jaxpr/dot_general | solution.py:45
  295.5 4.7 copy.15
  306.3 11.5 %fusion.33 = f32[32,32768]{1,0:T(8,128)} fusion(f32[32,32768]{1,0:T(8,128)} %fusion.32, f32[64,32768]{1,0:T(8,128)} %bitcast.23, f32[32,32768]{1,0:T(8,128)} %get-tuple-element.235, pred[]{:T(512)S(6)} %compare.3, s32[64]{0:T(128)S(1)} %dynamic_slice.44), kind=kOutput, calls=%fused_computation.3.clone.1 | convolution fusion | flops 145754112 | bytes 20971776 | tf_op jit(solution)/shard_map/while/body/eval_jaxpr/dot_general | solution.py:45
  323.7 4.7 copy.15
  334.5 11.5 %fusion.33 = f32[32,32768]{1,0:T(8,128)} fusion(f32[32,32768]{1,0:T(8,128)} %fusion.32, f32[64,32768]{1,0:T(8,128)} %bitcast.23, f32[32,32768]{1,0:T(8,128)} %get-tuple-element.235, pred[]{:T(512)S(6)} %compare.3, s32[64]{0:T(128)S(1)} %dynamic_slice.44), kind=kOutput, calls=%fused_computation.3.clone.1 | convolution fusion | flops 145754112 | bytes 20971776 | tf_op jit(solution)/shard_map/while/body/eval_jaxpr/dot_general | solution.py:45
  345.9 4.9 reshape.30
  351.4 90.0 %collective-permute-done = f32[4096,256]{1,0:T(8,128)S(1)} collective-permute-done((f32[4096,256]{1,0:T(8,128)}, f32[4096,256]{1,0:T(8,128)S(1)}, u32[]{:S(2)}, u32[]{:S(2)}) %collective-permute-start) | collective-permute-done | bytes 4194336 | tf_op jit(solution)/shard_map/ppermute | solution.py:12
  446.6 88.7 %collective-permute-done.1 = f32[4096,256]{1,0:T(8,128)S(1)} collective-permute-done((f32[4096,256]{1,0:T(8,128)S(1)}, f32[4096,256]{1,0:T(8,128)S(1)}, u32[]{:S(2)}, u32[]{:S(2)}) %collective-permute-start.1) | collective-permute-done | bytes 4194336 | tf_op jit(solution)/shard_map/ppermute | solution.py:12
  540.5 178.3 %collective-permute-done.2 = f32[4096,256]{1,0:T(8,128)} collective-permute-done((f32[4096,256]{1,0:T(8,128)}, f32[4096,256]{1,0:T(8,128)}, u32[]{:S(2)}, u32[]{:S(2)}) %collective-permute-start.2) | collective-permute-done | bytes 4194336 | tf_op jit(solution)/shard_map/ppermute | solution.py:12
  722.3 38.5 %psum.15 = f32[256]{0:T(256)} all-reduce(f32[256]{0:T(256)S(1)} %get-tuple-element.184), channel_id=1, replica_groups=mesh['grp'=4,'mem'=8] {'grp','mem'}, use_global_device_ids=true, to_apply=%region_4.0 | all-reduce | flops 256 | bytes 2048 | tf_op jit(solution)/shard_map/psum | solution.py:64
  760.7 88.4 %all-reduce.2.cloned.1.call-done = f32[256,256]{1,0:T(8,128)} async-done(((f32[256,256]{1,0:T(8,128)}), f32[256,256]{1,0:T(8,128)}) %all-reduce.2.cloned.1.call-update) | async-done | bytes 262160 | tf_op jit(solution)/shard_map/psum | solution.py:64
  (97 shorter events, 128.3 us)
Async XLA Ops:
  7.2 712.9 %copy-start = (bf16[256,256]{1,0:T(8,128)(2,1)S(1)}, bf16[256,256]{1,0:T(8,128)(2,1)}, u32[]{:S(2)}) copy-start(bf16[256,256]{1,0:T(8,128)(2,1)} %param.13) | copy-start | bytes 393220
  7.2 54.8 %all-gather.2.cloned.1.call-start = ((), (), s32[]{:S(2)}) async-start(), calls=%async_computation | async-start | bytes 2359296 | tf_op jit(solution)/shard_map/all_gather | solution.py:21
  7.9 841.2 %all-reduce.2.cloned.1.call-start = ((), (), s32[]{:S(2)}) async-start(), calls=%async_computation.1 | async-start | bytes 524288 | tf_op jit(solution)/shard_map/psum | solution.py:64
  75.6 3.2 copy-start.1
  102.7 3.2 copy-start.1
  130.9 3.2 copy-start.1
  159.1 3.2 copy-start.1
  187.3 3.2 copy-start.1
  215.6 3.2 copy-start.1
  243.8 3.2 copy-start.1
  272.0 3.2 copy-start.1
  300.2 3.2 copy-start.1
  328.5 3.2 copy-start.1
  350.8 90.6 %collective-permute-start = (f32[4096,256]{1,0:T(8,128)}, f32[4096,256]{1,0:T(8,128)S(1)}, u32[]{:S(2)}, u32[]{:S(2)}) collective-permute-start(f32[4096,256]{1,0:T(8,128)} %reshape.30), channel_id=1, source_target_pairs={{0,1},{1,0},{2,3},{3,2},{4,5},{5,4},{6,7},{7,6},{8,9},{9,8},{10,11... | collective-permute-start | bytes 12582920 | tf_op jit(solution)/shard_map/ppermute | solution.py:12
  444.2 275.9 %copy-start.2 = (bf16[512,256]{1,0:T(8,128)(2,1)S(1)}, bf16[512,256]{1,0:T(8,128)(2,1)}, u32[]{:S(2)}) copy-start(bf16[512,256]{1,0:T(8,128)(2,1)} %param.15) | copy-start | bytes 786436
  444.2 275.9 %copy-start.3 = (f32[256]{0:T(256)S(1)}, f32[256]{0:T(256)}, u32[]{:S(2)}) copy-start(f32[256]{0:T(256)} %param.14) | copy-start | bytes 3076
  444.2 91.1 %collective-permute-start.1 = (f32[4096,256]{1,0:T(8,128)S(1)}, f32[4096,256]{1,0:T(8,128)S(1)}, u32[]{:S(2)}, u32[]{:S(2)}) collective-permute-start(f32[4096,256]{1,0:T(8,128)S(1)} %add.69), channel_id=1, source_target_pairs={{0,2},{1,3},{2,0},{3,1},{4,6},{5,7},{6,4},{7,5},{8,10},{9,11},{10,... | collective-permute-start | bytes 12582920 | tf_op jit(solution)/shard_map/ppermute | solution.py:12
  537.8 181.1 %collective-permute-start.2 = (f32[4096,256]{1,0:T(8,128)}, f32[4096,256]{1,0:T(8,128)}, u32[]{:S(2)}, u32[]{:S(2)}) collective-permute-start(f32[4096,256]{1,0:T(8,128)} %add.70), channel_id=1, source_target_pairs={{0,4},{1,5},{2,6},{3,7},{4,0},{5,1},{6,2},{7,3},{8,12},{9,13},{10,... | collective-permute-start | bytes 12582920 | tf_op jit(solution)/shard_map/ppermute | solution.py:12
Sparse Core Ops, SparseCore 0:
  10.1 51.7 all-gather.1
  722.4 126.6 all-reduce.1
